TPU v7x, 256 devices: a whole 4x4x8 slice. The times are simulated.
256 devices in a mesh: sample: 16 (over z, x_hi), seq: 16 (over y, x_lo, core).
Axes of the slice: x: 4 (x_hi: 2, x_lo: 2; x = x_hi * 2 + x_lo), y: 4, z: 8, core: 2. Of those that a mesh axis runs over, the one named last changes fastest.
Arguments:
- queries: bfloat16 [16, 2048, 8192], P('sample', 'seq'), may hold values from -900 to 900
- span_keys: bfloat16 [16, 2048, 1024], P('sample', 'seq'), may hold values from -6 to 6
- span_values: bfloat16 [16, 2048, 1024], P('sample', 'seq'), may hold values from -6 to 6
- prompt_keys: bfloat16 [2048, 1024], P('sample'), may hold values from -6 to 6
- prompt_values: bfloat16 [2048, 1024], P('sample'), may hold values from -6 to 6
- lengths: int32 [16], P('sample'), may hold values from 512 to 8192, as said below
- offsets: int32 [16], P('sample'), may hold values from 0 to 6144, as said below
Outputs:
- attended: bfloat16 [16, 2048, 8192], P('sample', 'seq')
Inputs may be any that keep to these rules, and one draw needn't show every extreme that they name: A completion's block holds at least 512 live tokens: lengths[c] - offsets[c] >= 512. `offsets`: each offset is a whole multiple of 2048.
All inputs are finite; a program needn't handle non-finite values.
Results may differ from a plain program's by a relative error of at most 0.012.
The roundings to bfloat16 on the way count: a program that leaves them out, or rounds other values in their place, can miss the bound.
Values may be sent and summed in bfloat16 or wider, within the bound.
No kernel may reach another device: no remote copies, remote signals or barrier semaphores. Data moves between devices by JAX's collectives and lax.ppermute only.
A program may use at most 128 MiB of HBM per device.

v0:
```python
import math
import jax
import jax.numpy as jnp
from jax import lax
from jax.sharding import PartitionSpec as P

HEADS = 64
KV_HEADS = 8
HEAD_DIM = 128
ROPE_BASE = 500000.0
NEG_FILL = -1e30


def rope_angles(positions, head_size):
    half_dim = head_size // 2
    frequency = ROPE_BASE ** (-(jnp.arange(half_dim, dtype=jnp.float32) * (2.0 / head_size)))
    angles = positions.astype(jnp.float32)[:, None] * frequency[None, :]
    return (jnp.cos(angles), jnp.sin(angles))


def rotate(stacked, cos_table, sine_table):
    half_dim = stacked.shape[-1] // 2
    former = stacked[..., :half_dim]
    latter = stacked[..., half_dim:]
    cos_part = cos_table[:, None, :]
    sine_part = sine_table[:, None, :]
    return jnp.concatenate(
        [former * cos_part - latter * sine_part, latter * cos_part + former * sine_part], axis=-1
    )


def absorb(carry_state, query_group, key_rows, value_rows, allowed):
    run_max, run_sum, run_acc = carry_state
    scaling = 1.0 / math.sqrt(query_group.shape[-1])
    scores = (
        jnp.einsum("agqd,kad->agqk", query_group, key_rows, preferred_element_type=jnp.float32)
        * scaling
    )
    if allowed is not None:
        scores = jnp.where(allowed, scores, NEG_FILL)
    new_max = jnp.maximum(run_max, jnp.max(scores, axis=-1))
    weights = jnp.exp(scores - new_max[..., None])
    if allowed is not None:
        weights = jnp.where(allowed, weights, 0.0)
    fade_factor = jnp.exp(run_max - new_max)
    new_sum = run_sum * fade_factor + jnp.sum(weights, axis=-1)
    product = jnp.einsum(
        "agqk,kad->agqd",
        weights.astype(jnp.bfloat16),
        value_rows,
        preferred_element_type=jnp.float32,
    )
    return (new_max, new_sum, run_acc * fade_factor[..., None] + product)


def shards(queries, span_keys, span_values, prompt_keys, prompt_values, lengths, offsets):
    seq_count = lax.axis_size("seq")
    seq_index = lax.axis_index("seq")
    local_rows = queries.shape[1]
    span_len = local_rows * seq_count
    prompt_local = prompt_keys.shape[0]
    prompt_len = prompt_local * lax.axis_size("sample")
    group_size = HEADS // KV_HEADS
    length = lengths[0]
    offset = offsets[0]
    live_count = jnp.clip(length - offset, 0, span_len)
    row_ids = seq_index * local_rows + jnp.arange(local_rows, dtype=jnp.int32)
    cos_table, sine_table = rope_angles(prompt_len + offset + row_ids, HEAD_DIM)
    rotated_q = rotate(
        queries[0].astype(jnp.float32).reshape(local_rows, HEADS, HEAD_DIM), cos_table, sine_table
    ).astype(jnp.bfloat16)
    rotated_k = rotate(
        span_keys[0].astype(jnp.float32).reshape(local_rows, KV_HEADS, HEAD_DIM),
        cos_table,
        sine_table,
    ).astype(jnp.bfloat16)
    grouped = rotated_q.reshape(local_rows, KV_HEADS, 1, group_size, HEAD_DIM).transpose(
        1, 2, 3, 0, 4
    )
    initial = (
        jnp.full((KV_HEADS, 1, group_size, local_rows), NEG_FILL, jnp.float32),
        jnp.zeros((KV_HEADS, 1, group_size, local_rows), jnp.float32),
        jnp.zeros((KV_HEADS, 1, group_size, local_rows, HEAD_DIM), jnp.float32),
    )

    def by_head(carry_state, key_piece, value_piece, allowed):
        key_heads = key_piece.reshape(-1, KV_HEADS, 1, HEAD_DIM).transpose(1, 0, 2, 3)
        value_split = value_piece.reshape(-1, KV_HEADS, 1, HEAD_DIM).transpose(1, 0, 2, 3)

        def one_head(packed):
            query_head, run_max, run_sum, run_acc, key_head, value_head = packed
            return absorb((run_max, run_sum, run_acc), query_head, key_head, value_head, allowed)

        return lax.map(one_head, (grouped,) + tuple(carry_state) + (key_heads, value_split))

    shard_piece = (
        lax.all_gather(prompt_keys, "sample", axis=0, tiled=True),
        lax.all_gather(prompt_values, "sample", axis=0, tiled=True),
    )
    after_prompt = by_head(initial, shard_piece[0], shard_piece[1], None)
    last_row = seq_index * local_rows + local_rows - 1
    any_live = seq_index * local_rows < live_count
    flat_keys = rotated_k.reshape(local_rows, KV_HEADS * HEAD_DIM)
    shard_piece = (
        lax.all_gather(flat_keys, "seq", axis=0, tiled=True),
        lax.all_gather(span_values[0], "seq", axis=0, tiled=True),
    )
    piece_count = shard_piece[0].shape[0]
    key_ids = jnp.arange(piece_count, dtype=jnp.int32)
    allowed = (key_ids[None, :] <= row_ids[:, None]) & (key_ids < live_count)[None, :]
    needed = (jnp.int32(0) <= last_row) & any_live
    final_max, final_sum, final_acc = lax.cond(
        needed,
        lambda: tuple(by_head(after_prompt, shard_piece[0], shard_piece[1], allowed)),
        lambda: tuple(after_prompt),
    )
    safe_sum = jnp.where(final_sum > 0.0, final_sum, 1.0)
    outcome = (
        (final_acc / safe_sum[..., None])
        .transpose(3, 0, 1, 2, 4)
        .reshape(local_rows, HEADS * HEAD_DIM)
    )
    live_mask = row_ids < live_count
    outcome = jnp.where(live_mask[:, None], outcome, 0.0).astype(jnp.bfloat16)
    return outcome.reshape(1, local_rows, HEADS * HEAD_DIM)


def solution(mesh):
    in_specs = (
        P("sample", "seq", None),
        P("sample", "seq", None),
        P("sample", "seq", None),
        P("sample", None),
        P("sample", None),
        P("sample"),
        P("sample"),
    )
    out_specs = P("sample", "seq", None)
    return jax.shard_map(shards, mesh=mesh, in_specs=in_specs, out_specs=out_specs, check_vma=False)
```

profile of v0, /device:TPU:1, one launch (start us, length us, event | category | flops | bytes accessed | tf_op | source)
XLA Modules:
  0.0 418.2 jit_solution(11268256134059771003)
XLA Ops:
  17.9 4.9 %subtract_convert_fusion = (bf16[128,64,64]{2,0,1:T(8,128)(2,1)S(1)}, bf16[128,64,64]{2,0,1:T(8,128)(2,1)S(1)}) fusion(f32[128,64,64]{2,1,0:T(8,128)S(1)} %get-tuple-element.232, f32[128,64,64]{2,1,0:T(8,128)S(1)} %get-tuple-element.231, f32[128,64]{1,0:T(8,128)S(1)} %copy.30, f32[128,64]{1,0:T(8,128)S(1)} %copy.28), kind=kLoop, calls=%fused_computation.64 | loop fusion | flops 4194304 | bytes 6356992 | tf_op jit(solution)/shard_map/convert.7
  24.0 91.1 %all-gather.6.cloned.1.call-done = bf16[2048,1024]{0,1:T(8,128)(2,1)} async-done(((bf16[128,1024]{0,1:T(8,128)(2,1)}), bf16[2048,1024]{0,1:T(8,128)(2,1)}) %all-gather.6.cloned.1.call-update) | async-done | bytes 4194320 | tf_op jit(solution)/shard_map/all_gather | solution.py:97
  115.1 104.2 %all-gather.8.cloned.1.call-done = bf16[2048,1024]{0,1:T(8,128)(2,1)} async-done(((bf16[128,1024]{0,1:T(8,128)(2,1)}), bf16[2048,1024]{0,1:T(8,128)(2,1)}) %all-gather.8.cloned.1.call-update) | async-done | bytes 4194320 | tf_op jit(solution)/shard_map/all_gather | solution.py:98
  219.3 62.2 %while.26 = (s32[]{:T(128)}, f32[8,1,8,128]{3,2,1,0:T(8,128)S(1)}, f32[8,1,8,128]{3,2,1,0:T(8,128)S(1)}, f32[8,1,8,128,128]{4,3,2,1,0:T(8,128)}, bf16[8,1,8,128,...) while((s32[]{:T(128)}, f32[8,1,8,128]{3,2,1,0:T(8,128)S(1)}, ...), condition=%wide.region_3.4_spmd, body=%wide.region_0.3_spmd.sunk | while | flops 1090655232 | bytes 27052128 | solution.py:94
  223.4 3.7 fusion.77
  231.1 3.7 fusion.77
  234.8 2.4 multiply_reduce_fusion.2
  238.9 3.7 fusion.77
  242.6 2.4 multiply_reduce_fusion.2
  246.6 3.7 fusion.77
  250.4 2.4 multiply_reduce_fusion.2
  254.5 3.7 fusion.77
  258.2 2.4 multiply_reduce_fusion.2
  262.2 3.7 fusion.77
  270.0 3.7 fusion.77
  273.7 2.4 multiply_reduce_fusion.2
  277.8 3.7 fusion.77
  281.5 38.5 %all-gather.12.cloned.1.call-done = bf16[1,2048,1024]{1,2,0:T(8,128)(2,1)} async-done(((bf16[1,128,1024]{1,2,0:T(8,128)(2,1)}), bf16[1,2048,1024]{1,2,0:T(8,128)(2,1)}) %all-gather.12.cloned.1.call-update) | async-done | bytes 4194320 | tf_op jit(solution)/shard_map/all_gather | solution.py:106
  320.1 81.3 %conditional.1 = ((f32[8,1,8,128]{3,2,1,0:T(8,128)S(1)}, f32[8,1,8,128,128]{4,3,2,1,0:T(8,128)})) conditional(s32[]{:T(128)} %convert_element_type.55, (f32[8,1,8,128]{3,2,1,0:T(8,128)S(1)}, f32[8,1,8,128,128]{4,3,2,1,0:T(8,128)}) %tuple.21, (bf16[2048,1024]{0,1:T(8,128)(2,1)}, bf16[2048,1024]{0,1:T(8,128)(2,1)}, s32[]{:T(128)}, ...), branch_computations={%region_4.5_spmd, %region_5.10_spmd} | conditional | flops 1101797504 | bytes 38149884 | solution.py:112
  320.4 76.4 %while.25 = (s32[]{:T(128)}, f32[8,1,8,128]{3,2,1,0:T(8,128)S(1)}, f32[8,1,8,128,128]{4,3,2,1,0:T(8,128)}, f32[8,1,8,128]{3,2,1,0:T(8,128)S(1)}, f32[8,1,8,128]{...) while((s32[]{:T(128)}, f32[8,1,8,128]{3,2,1,0:T(8,128)S(1)}, ...), condition=%wide.region_9.9_spmd, body=%wide.region_6.8_spmd.sunk | while | flops 1101271040 | bytes 28371068 | solution.py:94
  320.5 2.7 fusion.80
  323.2 2.5 fusion.82
  325.7 4.3 %fusion.84 = f32[8,1,8,128,128]{4,3,2,1,0:T(8,128)} fusion(f32[8,1,8,128,128]{4,3,2,1,0:T(8,128)} %get-tuple-element.374, s32[]{:T(128)S(6)} %copy.59, f32[8,128,2048]{2,1,0:T(8,128)S(1)} %get-tuple-element.357, f32[8,128]{1,0:T(8,128)S(1)} %get-tuple-element.359, pred[128,2048]{1,0:T(8,128)(4,1)S(1)} %get-tuple-element.388, ...), kind=kOutput, calls=%fused_computation.35.clone.1 | convolution fusion | flops 547618816 | bytes 10232832 | tf_op jit(solution)/shard_map/cond/branch_1_fun/while/body/eval_jaxpr/agqk,kad->agqd/dot_general | solution.py:47
  330.0 2.7 fusion.80
  332.7 2.5 fusion.82
  335.2 4.3 %fusion.84 = f32[8,1,8,128,128]{4,3,2,1,0:T(8,128)} fusion(f32[8,1,8,128,128]{4,3,2,1,0:T(8,128)} %get-tuple-element.374, s32[]{:T(128)S(6)} %copy.59, f32[8,128,2048]{2,1,0:T(8,128)S(1)} %get-tuple-element.357, f32[8,128]{1,0:T(8,128)S(1)} %get-tuple-element.359, pred[128,2048]{1,0:T(8,128)(4,1)S(1)} %get-tuple-element.388, ...), kind=kOutput, calls=%fused_computation.35.clone.1 | convolution fusion | flops 547618816 | bytes 10232832 | tf_op jit(solution)/shard_map/cond/branch_1_fun/while/body/eval_jaxpr/agqk,kad->agqd/dot_general | solution.py:47
  339.6 2.7 fusion.80
  342.3 2.5 fusion.82
  344.8 4.3 %fusion.84 = f32[8,1,8,128,128]{4,3,2,1,0:T(8,128)} fusion(f32[8,1,8,128,128]{4,3,2,1,0:T(8,128)} %get-tuple-element.374, s32[]{:T(128)S(6)} %copy.59, f32[8,128,2048]{2,1,0:T(8,128)S(1)} %get-tuple-element.357, f32[8,128]{1,0:T(8,128)S(1)} %get-tuple-element.359, pred[128,2048]{1,0:T(8,128)(4,1)S(1)} %get-tuple-element.388, ...), kind=kOutput, calls=%fused_computation.35.clone.1 | convolution fusion | flops 547618816 | bytes 10232832 | tf_op jit(solution)/shard_map/cond/branch_1_fun/while/body/eval_jaxpr/agqk,kad->agqd/dot_general | solution.py:47
  349.1 2.7 fusion.80
  351.8 2.5 fusion.82
  354.3 4.3 %fusion.84 = f32[8,1,8,128,128]{4,3,2,1,0:T(8,128)} fusion(f32[8,1,8,128,128]{4,3,2,1,0:T(8,128)} %get-tuple-element.374, s32[]{:T(128)S(6)} %copy.59, f32[8,128,2048]{2,1,0:T(8,128)S(1)} %get-tuple-element.357, f32[8,128]{1,0:T(8,128)S(1)} %get-tuple-element.359, pred[128,2048]{1,0:T(8,128)(4,1)S(1)} %get-tuple-element.388, ...), kind=kOutput, calls=%fused_computation.35.clone.1 | convolution fusion | flops 547618816 | bytes 10232832 | tf_op jit(solution)/shard_map/cond/branch_1_fun/while/body/eval_jaxpr/agqk,kad->agqd/dot_general | solution.py:47
  358.6 2.7 fusion.80
  361.3 2.5 fusion.82
  363.9 4.3 %fusion.84 = f32[8,1,8,128,128]{4,3,2,1,0:T(8,128)} fusion(f32[8,1,8,128,128]{4,3,2,1,0:T(8,128)} %get-tuple-element.374, s32[]{:T(128)S(6)} %copy.59, f32[8,128,2048]{2,1,0:T(8,128)S(1)} %get-tuple-element.357, f32[8,128]{1,0:T(8,128)S(1)} %get-tuple-element.359, pred[128,2048]{1,0:T(8,128)(4,1)S(1)} %get-tuple-element.388, ...), kind=kOutput, calls=%fused_computation.35.clone.1 | convolution fusion | flops 547618816 | bytes 10232832 | tf_op jit(solution)/shard_map/cond/branch_1_fun/while/body/eval_jaxpr/agqk,kad->agqd/dot_general | solution.py:47
  368.2 2.7 fusion.80
  370.9 2.5 fusion.82
  373.4 4.3 %fusion.84 = f32[8,1,8,128,128]{4,3,2,1,0:T(8,128)} fusion(f32[8,1,8,128,128]{4,3,2,1,0:T(8,128)} %get-tuple-element.374, s32[]{:T(128)S(6)} %copy.59, f32[8,128,2048]{2,1,0:T(8,128)S(1)} %get-tuple-element.357, f32[8,128]{1,0:T(8,128)S(1)} %get-tuple-element.359, pred[128,2048]{1,0:T(8,128)(4,1)S(1)} %get-tuple-element.388, ...), kind=kOutput, calls=%fused_computation.35.clone.1 | convolution fusion | flops 547618816 | bytes 10232832 | tf_op jit(solution)/shard_map/cond/branch_1_fun/while/body/eval_jaxpr/agqk,kad->agqd/dot_general | solution.py:47
  377.7 2.7 fusion.80
  380.4 2.5 fusion.82
  383.0 4.3 %fusion.84 = f32[8,1,8,128,128]{4,3,2,1,0:T(8,128)} fusion(f32[8,1,8,128,128]{4,3,2,1,0:T(8,128)} %get-tuple-element.374, s32[]{:T(128)S(6)} %copy.59, f32[8,128,2048]{2,1,0:T(8,128)S(1)} %get-tuple-element.357, f32[8,128]{1,0:T(8,128)S(1)} %get-tuple-element.359, pred[128,2048]{1,0:T(8,128)(4,1)S(1)} %get-tuple-element.388, ...), kind=kOutput, calls=%fused_computation.35.clone.1 | convolution fusion | flops 547618816 | bytes 10232832 | tf_op jit(solution)/shard_map/cond/branch_1_fun/while/body/eval_jaxpr/agqk,kad->agqd/dot_general | solution.py:47
  387.3 2.7 fusion.80
  390.0 2.5 fusion.82
  392.5 4.3 %fusion.84 = f32[8,1,8,128,128]{4,3,2,1,0:T(8,128)} fusion(f32[8,1,8,128,128]{4,3,2,1,0:T(8,128)} %get-tuple-element.374, s32[]{:T(128)S(6)} %copy.59, f32[8,128,2048]{2,1,0:T(8,128)S(1)} %get-tuple-element.357, f32[8,128]{1,0:T(8,128)S(1)} %get-tuple-element.359, pred[128,2048]{1,0:T(8,128)(4,1)S(1)} %get-tuple-element.388, ...), kind=kOutput, calls=%fused_computation.35.clone.1 | convolution fusion | flops 547618816 | bytes 10232832 | tf_op jit(solution)/shard_map/cond/branch_1_fun/while/body/eval_jaxpr/agqk,kad->agqd/dot_general | solution.py:47
  396.8 4.6 %copy.80 = f32[8,1,8,128,128]{4,3,2,1,0:T(8,128)} copy(f32[8,1,8,128,128]{4,3,2,1,0:T(8,128)} %get-tuple-element.421) | data formatting | bytes 8388608 | tf_op jit(solution)/shard_map/cond
  401.5 2.9 divide_bitcast_fusion
  404.3 2.7 copy.38
  407.0 2.8 reshape.318
  (86 shorter events, 33.9 us)
Async XLA Ops:
  6.5 6.8 %copy-start.1 = (bf16[1,128,1024]{2,1,0:T(8,128)(2,1)S(1)}, bf16[1,128,1024]{2,1,0:T(8,128)(2,1)}, u32[]{:S(2)}) copy-start(bf16[1,128,1024]{2,1,0:T(8,128)(2,1)} %param.15) | copy-start | bytes 786436
  6.5 8.5 %copy-start = (bf16[1,128,8192]{2,1,0:T(8,128)(2,1)S(1)}, bf16[1,128,8192]{2,1,0:T(8,128)(2,1)}, u32[]{:S(2)}) copy-start(bf16[1,128,8192]{2,1,0:T(8,128)(2,1)} %param.13) | copy-start | bytes 6291460
  6.5 108.5 %all-gather.6.cloned.1.call-start = ((), (), s32[]{:S(2)}) async-start(), calls=%async_computation | async-start | bytes 4456448 | tf_op jit(solution)/shard_map/all_gather | solution.py:97
  8.5 210.8 %all-gather.8.cloned.1.call-start = ((), (), s32[]{:S(2)}) async-start(), calls=%async_computation.1 | async-start | bytes 4456448 | tf_op jit(solution)/shard_map/all_gather | solution.py:98
  10.4 271.1 %all-gather.10.cloned.1.call-start = ((), (), s32[]{:S(2)}) async-start(), calls=%async_computation.2 | async-start | bytes 4456448 | tf_op jit(solution)/shard_map/all_gather | solution.py:105
  13.2 306.8 %all-gather.12.cloned.1.call-start = ((), (), s32[]{:S(2)}) async-start(), calls=%async_computation.3 | async-start | bytes 4456448 | tf_op jit(solution)/shard_map/all_gather | solution.py:106
Sparse Core Ops, SparseCore 0:
  9.8 105.2 all-gather.5
  117.5 101.7 all-gather.7
  221.1 49.3 all-gather.9
  272.1 47.8 all-gather.11
where the time goes:
time: 420 us; the launch traced here: 418 us
  waiting for transfers between devices  234 us (56%)
  matrix products  105 us (25%)
  other arithmetic  46 us (11%)
  local copies, waits for them, and re-layouts  18.5 us (4%)
  between operations  14.6 us (3%)
    all_gather x1, waiting for transfers between devices, shards(): lax.all_gather(prompt_values, 'sample', axis=0, tiled=True)  104 us
    all_gather x1, waiting for transfers between devices, shards(): lax.all_gather(prompt_keys, 'sample', axis=0, tiled=True)  91.1 us
    dot_general x16, matrix products, absorb(): jnp.einsum('agqk,kad->agqd', weights.astype(jnp.bfloat16), value_rows, pr...  64.2 us
    dot_general x16, matrix products, absorb(): jnp.einsum('agqd,kad->agqk', query_group, key_rows, preferred_element_typ...  40.5 us
    all_gather x1, waiting for transfers between devices, shards(): lax.all_gather(span_values[0], 'seq', axis=0, tiled=True)  38.5 us
    reduce_sum x16, other arithmetic, absorb(): new_sum = run_sum * fade_factor + jnp.sum(weights, axis=-1)  33.2 us
  transfers between devices with their start and end apart: 4, of which 3 were waited for; matrix products, arithmetic and copies ran while one was open for 18% of the time, Pallas kernels for 0%

commit v1 on v0

--- a/solution.py
+++ b/solution.py
@@ -9,6 +9,13 @@
 HEAD_DIM = 128
 ROPE_BASE = 500000.0
 NEG_FILL = -1e30
+
+
+def swapped_in(shard, axis, dim):
+    size = lax.axis_size(axis)
+    blocks = jnp.stack([shard for _ in range(size)])
+    blocks = lax.all_to_all(blocks, axis, split_axis=0, concat_axis=0)
+    return jnp.concatenate(blocks, axis=dim)
 
 
 def rope_angles(positions, head_size):
@@ -94,7 +101,7 @@
         return lax.map(one_head, (grouped,) + tuple(carry_state) + (key_heads, value_split))
 
     shard_piece = (
-        lax.all_gather(prompt_keys, "sample", axis=0, tiled=True),
+        swapped_in(prompt_keys, "sample", 0),
         lax.all_gather(prompt_values, "sample", axis=0, tiled=True),
     )
     after_prompt = by_head(initial, shard_piece[0], shard_piece[1], None)

time: 420 us -> 380 us (0.905)
  waiting for transfers between devices: 234 us -> 175 us
  starting transfers between devices: 0.13 us -> 11.8 us
  local copies, waits for them, and re-layouts: 18.5 us -> 25.9 us
    all_to_all x0 -> x1, waiting for transfers between devices: none -> 98.2 us  [swapped_in(): blocks = lax.all_to_all(blocks, axis, split_axis=0, concat_axis=0)]
    all_gather x1 -> x0, waiting for transfers between devices: 91.1 us -> none  [shards(): lax.all_gather(prompt_keys, 'sample', axis=0, tiled=True)]
    all_gather x1, waiting for transfers between devices: 104 us -> 37.2 us  [shards(): lax.all_gather(prompt_values, 'sample', axis=0, tiled=True)]
    all_to_all x0 -> x1, starting transfers between devices: none -> 11.8 us  [swapped_in(): blocks = lax.all_to_all(blocks, axis, split_axis=0, concat_axis=0)]
  transfers between devices with their start and end apart: 4 -> 4, of which waited for: 3 -> 3; matrix products, arithmetic and copies ran while one was open for 18% -> 22% of each run, Pallas kernels for 0% -> 0%
where the time goes in v1:
time: 380 us; the launch traced here: 378 us
  waiting for transfers between devices  175 us (46%)
  matrix products  105 us (28%)
  other arithmetic  46.1 us (12%)
  local copies, waits for them, and re-layouts  25.9 us (7%)
  between operations  14.6 us (4%)
  starting transfers between devices  11.8 us (3%)
    all_to_all x1, waiting for transfers between devices, swapped_in(): blocks = lax.all_to_all(blocks, axis, split_axis=0, concat_axis=0)  98.2 us
    dot_general x16, matrix products, absorb(): jnp.einsum('agqk,kad->agqd', weights.astype(jnp.bfloat16), value_rows, pr...  64.6 us
    dot_general x16, matrix products, absorb(): jnp.einsum('agqd,kad->agqk', query_group, key_rows, preferred_element_typ...  40.4 us
    all_gather x1, waiting for transfers between devices, shards(): lax.all_gather(span_values[0], 'seq', axis=0, tiled=True)  39.2 us
    all_gather x1, waiting for transfers between devices, shards(): lax.all_gather(prompt_values, 'sample', axis=0, tiled=True)  37.2 us
    reduce_sum x16, other arithmetic, absorb(): new_sum = run_sum * fade_factor + jnp.sum(weights, axis=-1)  33.2 us
    all_to_all x1, starting transfers between devices, swapped_in(): blocks = lax.all_to_all(blocks, axis, split_axis=0, concat_axis=0)  11.8 us
  transfers between devices with their start and end apart: 4, of which 3 were waited for; matrix products, arithmetic and copies ran while one was open for 22% of the time, Pallas kernels for 0%

profile of v1, /device:TPU:1, one launch (start us, length us, event | category | flops | bytes accessed | tf_op | source)
XLA Modules:
  0.0 378.5 jit_solution(8683975034971782056)
XLA Ops:
  11.2 3.4 stack.2
  14.7 11.8 %all-to-all-start = ((bf16[16,128,1024]{2,1,0:T(8,128)(2,1)}), bf16[16,128,1024]{2,1,0:T(8,128)(2,1)}, u32[]{:S(2)}, u32[]{:S(2)}) async-start(bf16[16,128,1024]{2,1,0:T(8,128)(2,1)} %stack.2), calls=%async_computation | async-start | bytes 8388608 | tf_op jit(solution)/shard_map/all_to_all | solution.py:17
  31.1 4.9 %subtract_convert_fusion = (bf16[128,64,64]{2,0,1:T(8,128)(2,1)S(1)}, bf16[128,64,64]{2,0,1:T(8,128)(2,1)S(1)}) fusion(f32[128,64,64]{2,1,0:T(8,128)S(1)} %get-tuple-element.232, f32[128,64,64]{2,1,0:T(8,128)S(1)} %get-tuple-element.231, f32[128,64]{1,0:T(8,128)S(1)} %copy.29, f32[128,64]{1,0:T(8,128)S(1)} %copy.27), kind=kLoop, calls=%fused_computation.64 | loop fusion | flops 4194304 | bytes 6356992 | tf_op jit(solution)/shard_map/convert.7
  37.2 98.2 %all-to-all-done = bf16[16,128,1024]{2,1,0:T(8,128)(2,1)} async-done(((bf16[16,128,1024]{2,1,0:T(8,128)(2,1)}), bf16[16,128,1024]{2,1,0:T(8,128)(2,1)}, u32[]{:S(2)}, u32[]{:S(2)}) %all-to-all-start) | async-done | bytes 4194336 | tf_op jit(solution)/shard_map/all_to_all | solution.py:17
  135.4 3.3 copy.44
  138.7 2.6 copy.31
  141.3 37.2 %all-gather.5.cloned.1.call-done = bf16[2048,1024]{0,1:T(8,128)(2,1)} async-done(((bf16[128,1024]{0,1:T(8,128)(2,1)}), bf16[2048,1024]{0,1:T(8,128)(2,1)}) %all-gather.5.cloned.1.call-update) | async-done | bytes 4194320 | tf_op jit(solution)/shard_map/all_gather | solution.py:105
  178.5 62.3 %while.26 = (s32[]{:T(128)}, f32[8,1,8,128]{3,2,1,0:T(8,128)S(1)}, f32[8,1,8,128]{3,2,1,0:T(8,128)S(1)}, f32[8,1,8,128,128]{4,3,2,1,0:T(8,128)}, bf16[8,1,8,128,...) while((s32[]{:T(128)}, f32[8,1,8,128]{3,2,1,0:T(8,128)S(1)}, ...), condition=%wide.region_3.4_spmd, body=%wide.region_0.3_spmd.sunk | while | flops 1090655232 | bytes 27052128 | solution.py:101
  182.6 3.7 fusion.77
  186.3 2.4 multiply_reduce_fusion.2
  190.3 3.7 fusion.77
  198.1 3.8 fusion.77
  205.9 3.7 fusion.77
  213.7 3.8 %fusion.77 = f32[8,1,8,128,128]{4,3,2,1,0:T(8,128)} fusion(f32[8,1,8,128,128]{4,3,2,1,0:T(8,128)} %get-tuple-element.405, s32[]{:T(128)S(6)} %copy.67, f32[8,128,2048]{2,1,0:T(8,128)S(1)} %get-tuple-element.341, f32[8,128]{1,0:T(8,128)S(1)} %get-tuple-element.343, bf16[8,2048,1,128]{1,3,0,2:T(8,128)(2,1)} %get-tuple-element.416, ...), kind=kOutput, calls=%fused_computation.7.clone.1 | convolution fusion | flops 543293440 | bytes 9446400 | tf_op jit(solution)/shard_map/while/body/eval_jaxpr/agqk,kad->agqd/dot_general | solution.py:54
  221.5 3.7 fusion.77
  229.3 3.7 fusion.77
  237.1 3.7 fusion.77
  240.8 39.2 %all-gather.9.cloned.1.call-done = bf16[1,2048,1024]{1,2,0:T(8,128)(2,1)} async-done(((bf16[1,128,1024]{1,2,0:T(8,128)(2,1)}), bf16[1,2048,1024]{1,2,0:T(8,128)(2,1)}) %all-gather.9.cloned.1.call-update) | async-done | bytes 4194320 | tf_op jit(solution)/shard_map/all_gather | solution.py:113
  280.2 81.6 %conditional.1 = ((f32[8,1,8,128]{3,2,1,0:T(8,128)S(1)}, f32[8,1,8,128,128]{4,3,2,1,0:T(8,128)})) conditional(s32[]{:T(128)} %convert_element_type.55, (f32[8,1,8,128]{3,2,1,0:T(8,128)S(1)}, f32[8,1,8,128,128]{4,3,2,1,0:T(8,128)}) %tuple.21, (bf16[2048,1024]{0,1:T(8,128)(2,1)}, bf16[2048,1024]{0,1:T(8,128)(2,1)}, s32[]{:T(128)}, ...), branch_computations={%region_4.5_spmd, %region_5.10_spmd} | conditional | flops 1101797504 | bytes 38149884 | solution.py:119
  280.5 76.6 %while.25 = (s32[]{:T(128)}, f32[8,1,8,128]{3,2,1,0:T(8,128)S(1)}, f32[8,1,8,128,128]{4,3,2,1,0:T(8,128)}, f32[8,1,8,128]{3,2,1,0:T(8,128)S(1)}, f32[8,1,8,128]{...) while((s32[]{:T(128)}, f32[8,1,8,128]{3,2,1,0:T(8,128)S(1)}, ...), condition=%wide.region_9.9_spmd, body=%wide.region_6.8_spmd.sunk | while | flops 1101271040 | bytes 28371068 | solution.py:101
  280.5 2.7 fusion.80
  283.2 2.5 fusion.82
  285.8 4.3 %fusion.84 = f32[8,1,8,128,128]{4,3,2,1,0:T(8,128)} fusion(f32[8,1,8,128,128]{4,3,2,1,0:T(8,128)} %get-tuple-element.374, s32[]{:T(128)S(6)} %copy.57, f32[8,128,2048]{2,1,0:T(8,128)S(1)} %get-tuple-element.357, f32[8,128]{1,0:T(8,128)S(1)} %get-tuple-element.359, pred[128,2048]{1,0:T(8,128)(4,1)S(1)} %get-tuple-element.388, ...), kind=kOutput, calls=%fused_computation.35.clone.1 | convolution fusion | flops 547618816 | bytes 10232832 | tf_op jit(solution)/shard_map/cond/branch_1_fun/while/body/eval_jaxpr/agqk,kad->agqd/dot_general | solution.py:54
  290.1 2.7 fusion.80
  292.8 2.5 fusion.82
  295.3 4.3 %fusion.84 = f32[8,1,8,128,128]{4,3,2,1,0:T(8,128)} fusion(f32[8,1,8,128,128]{4,3,2,1,0:T(8,128)} %get-tuple-element.374, s32[]{:T(128)S(6)} %copy.57, f32[8,128,2048]{2,1,0:T(8,128)S(1)} %get-tuple-element.357, f32[8,128]{1,0:T(8,128)S(1)} %get-tuple-element.359, pred[128,2048]{1,0:T(8,128)(4,1)S(1)} %get-tuple-element.388, ...), kind=kOutput, calls=%fused_computation.35.clone.1 | convolution fusion | flops 547618816 | bytes 10232832 | tf_op jit(solution)/shard_map/cond/branch_1_fun/while/body/eval_jaxpr/agqk,kad->agqd/dot_general | solution.py:54
  299.7 2.7 fusion.80
  302.4 2.5 fusion.82
  304.9 4.3 %fusion.84 = f32[8,1,8,128,128]{4,3,2,1,0:T(8,128)} fusion(f32[8,1,8,128,128]{4,3,2,1,0:T(8,128)} %get-tuple-element.374, s32[]{:T(128)S(6)} %copy.57, f32[8,128,2048]{2,1,0:T(8,128)S(1)} %get-tuple-element.357, f32[8,128]{1,0:T(8,128)S(1)} %get-tuple-element.359, pred[128,2048]{1,0:T(8,128)(4,1)S(1)} %get-tuple-element.388, ...), kind=kOutput, calls=%fused_computation.35.clone.1 | convolution fusion | flops 547618816 | bytes 10232832 | tf_op jit(solution)/shard_map/cond/branch_1_fun/while/body/eval_jaxpr/agqk,kad->agqd/dot_general | solution.py:54
  309.3 2.7 fusion.80
  312.0 2.5 fusion.82
  314.5 4.3 %fusion.84 = f32[8,1,8,128,128]{4,3,2,1,0:T(8,128)} fusion(f32[8,1,8,128,128]{4,3,2,1,0:T(8,128)} %get-tuple-element.374, s32[]{:T(128)S(6)} %copy.57, f32[8,128,2048]{2,1,0:T(8,128)S(1)} %get-tuple-element.357, f32[8,128]{1,0:T(8,128)S(1)} %get-tuple-element.359, pred[128,2048]{1,0:T(8,128)(4,1)S(1)} %get-tuple-element.388, ...), kind=kOutput, calls=%fused_computation.35.clone.1 | convolution fusion | flops 547618816 | bytes 10232832 | tf_op jit(solution)/shard_map/cond/branch_1_fun/while/body/eval_jaxpr/agqk,kad->agqd/dot_general | solution.py:54
  318.8 2.7 fusion.80
  321.5 2.5 fusion.82
  324.1 4.3 %fusion.84 = f32[8,1,8,128,128]{4,3,2,1,0:T(8,128)} fusion(f32[8,1,8,128,128]{4,3,2,1,0:T(8,128)} %get-tuple-element.374, s32[]{:T(128)S(6)} %copy.57, f32[8,128,2048]{2,1,0:T(8,128)S(1)} %get-tuple-element.357, f32[8,128]{1,0:T(8,128)S(1)} %get-tuple-element.359, pred[128,2048]{1,0:T(8,128)(4,1)S(1)} %get-tuple-element.388, ...), kind=kOutput, calls=%fused_computation.35.clone.1 | convolution fusion | flops 547618816 | bytes 10232832 | tf_op jit(solution)/shard_map/cond/branch_1_fun/while/body/eval_jaxpr/agqk,kad->agqd/dot_general | solution.py:54
  328.4 2.7 fusion.80
  331.1 2.5 fusion.82
  333.6 4.4 %fusion.84 = f32[8,1,8,128,128]{4,3,2,1,0:T(8,128)} fusion(f32[8,1,8,128,128]{4,3,2,1,0:T(8,128)} %get-tuple-element.374, s32[]{:T(128)S(6)} %copy.57, f32[8,128,2048]{2,1,0:T(8,128)S(1)} %get-tuple-element.357, f32[8,128]{1,0:T(8,128)S(1)} %get-tuple-element.359, pred[128,2048]{1,0:T(8,128)(4,1)S(1)} %get-tuple-element.388, ...), kind=kOutput, calls=%fused_computation.35.clone.1 | convolution fusion | flops 547618816 | bytes 10232832 | tf_op jit(solution)/shard_map/cond/branch_1_fun/while/body/eval_jaxpr/agqk,kad->agqd/dot_general | solution.py:54
  338.0 2.7 fusion.80
  340.7 2.5 fusion.82
  343.2 4.3 %fusion.84 = f32[8,1,8,128,128]{4,3,2,1,0:T(8,128)} fusion(f32[8,1,8,128,128]{4,3,2,1,0:T(8,128)} %get-tuple-element.374, s32[]{:T(128)S(6)} %copy.57, f32[8,128,2048]{2,1,0:T(8,128)S(1)} %get-tuple-element.357, f32[8,128]{1,0:T(8,128)S(1)} %get-tuple-element.359, pred[128,2048]{1,0:T(8,128)(4,1)S(1)} %get-tuple-element.388, ...), kind=kOutput, calls=%fused_computation.35.clone.1 | convolution fusion | flops 547618816 | bytes 10232832 | tf_op jit(solution)/shard_map/cond/branch_1_fun/while/body/eval_jaxpr/agqk,kad->agqd/dot_general | solution.py:54
  347.6 2.7 fusion.80
  350.3 2.5 fusion.82
  352.8 4.3 %fusion.84 = f32[8,1,8,128,128]{4,3,2,1,0:T(8,128)} fusion(f32[8,1,8,128,128]{4,3,2,1,0:T(8,128)} %get-tuple-element.374, s32[]{:T(128)S(6)} %copy.57, f32[8,128,2048]{2,1,0:T(8,128)S(1)} %get-tuple-element.357, f32[8,128]{1,0:T(8,128)S(1)} %get-tuple-element.359, pred[128,2048]{1,0:T(8,128)(4,1)S(1)} %get-tuple-element.388, ...), kind=kOutput, calls=%fused_computation.35.clone.1 | convolution fusion | flops 547618816 | bytes 10232832 | tf_op jit(solution)/shard_map/cond/branch_1_fun/while/body/eval_jaxpr/agqk,kad->agqd/dot_general | solution.py:54
  357.1 4.6 %copy.78 = f32[8,1,8,128,128]{4,3,2,1,0:T(8,128)} copy(f32[8,1,8,128,128]{4,3,2,1,0:T(8,128)} %get-tuple-element.421) | data formatting | bytes 8388608 | tf_op jit(solution)/shard_map/cond
  361.8 2.9 divide_bitcast_fusion
  364.7 2.7 copy.36
  367.3 2.8 reshape.316
  (87 shorter events, 41.4 us)
Async XLA Ops:
  6.5 172.0 %all-gather.5.cloned.1.call-start = ((), (), s32[]{:S(2)}) async-start(), calls=%async_computation.1 | async-start | bytes 4456448 | tf_op jit(solution)/shard_map/all_gather | solution.py:105
  8.4 232.5 %all-gather.7.cloned.1.call-start = ((), (), s32[]{:S(2)}) async-start(), calls=%async_computation.2 | async-start | bytes 4456448 | tf_op jit(solution)/shard_map/all_gather | solution.py:112
  14.7 11.8 %copy-start.1 = (bf16[1,128,1024]{2,1,0:T(8,128)(2,1)S(1)}, bf16[1,128,1024]{2,1,0:T(8,128)(2,1)}, u32[]{:S(2)}) copy-start(bf16[1,128,1024]{2,1,0:T(8,128)(2,1)} %param.15) | copy-start | bytes 786436
  14.7 13.6 %copy-start = (bf16[1,128,8192]{2,1,0:T(8,128)(2,1)S(1)}, bf16[1,128,8192]{2,1,0:T(8,128)(2,1)}, u32[]{:S(2)}) copy-start(bf16[1,128,8192]{2,1,0:T(8,128)(2,1)} %param.13) | copy-start | bytes 6291460
  14.7 120.7 %all-to-all-start = ((bf16[16,128,1024]{2,1,0:T(8,128)(2,1)}), bf16[16,128,1024]{2,1,0:T(8,128)(2,1)}, u32[]{:S(2)}, u32[]{:S(2)}) async-start(bf16[16,128,1024]{2,1,0:T(8,128)(2,1)} %stack.2), calls=%async_computation | async-start | bytes 8388608 | tf_op jit(solution)/shard_map/all_to_all | solution.py:17
  26.4 253.6 %all-gather.9.cloned.1.call-start = ((), (), s32[]{:S(2)}) async-start(), calls=%async_computation.3 | async-start | bytes 4456448 | tf_op jit(solution)/shard_map/all_gather | solution.py:113
Sparse Core Ops, SparseCore 0:
  9.8 168.6 all-gather.4
  180.2 50.2 all-gather.6
  232.3 47.7 all-gather.8
